TPU v7x, 32 devices: a whole 2x2x4 slice. The times are simulated.
32 devices in a mesh: grp: 2 (over x), slc: 16 (over z, y, core).
Axes of the slice: x: 2, y: 2, z: 4, core: 2. Of those that a mesh axis runs over, the one named last changes fastest.
Arguments:
- bitstrings: int32 [1024], P('grp'), parts along dimension 0, may hold values from 0 to 511, as said below
- tree_order: int32 [12], P('grp'), parts along dimension 0, may hold values from 0 to 5, each once
- owners: int32 [12], P('grp'), parts along dimension 0, may hold values from 0 to 15
- slice_assign: int32 [64, 6], P(('grp', 'slc')), parts along dimension 0, may hold values from 0 to 63
- boundary: bfloat16 [1024, 4096], P('grp'), parts along dimension 0, may hold values from -6 to 6
- branch_pool: bfloat16 [32, 64, 4096], P(('grp', 'slc')), parts along dimension 0, may hold values from -0.75 to 0.75
- slice_tensors: bfloat16 [12, 64, 4096], P('grp'), parts along dimension 0, may hold values from -3 to 3
- closing: bfloat16 [8192, 128], P('grp'), parts along dimension 0, may hold values from -0.09375 to 0.09375
Outputs:
- amplitudes: float32 [1024, 128], P(('grp', 'slc')), parts along dimension 0
There are 2 independent parts, one for each index of `grp`. A program takes and returns all parts, laid end to end along the dimension named above; each array names one. Nothing has to cross between parts.
Inputs may be any that keep to these rules, and one draw needn't show every extreme that they name: `bitstrings`: 512 distinct configurations. `tree_order`: a permutation of the sections.
All inputs are finite; a program needn't handle non-finite values.
Results may differ from a plain program's by a relative error of at most 0.0075.
Values may be sent and summed in bfloat16 or wider, within the bound.
A program may use at most 128 MiB of HBM per device.

v0:
```python
import math
import jax
import jax.numpy as jnp
from jax import lax
from jax.sharding import PartitionSpec as P


def spread(block, axis, owner):
    block = jnp.where(lax.axis_index(axis) == owner, block, jnp.zeros_like(block))
    return lax.psum(block, axis)


def local(
    bitstrings, tree_order, owners, slice_assign, boundary, branch_pool, slice_tensors, closing
):
    group_count = lax.axis_size("slc")
    my_index = lax.axis_index("slc")
    slice_count = slice_assign.shape[0]
    bond_dim = branch_pool.shape[1]
    pair_dim = branch_pool.shape[2]
    row_total = bitstrings.shape[0]
    section_count = tree_order.shape[0]
    starts = jnp.take(boundary, bitstrings, axis=0)
    states = jnp.broadcast_to(starts[None], (slice_count, row_total, pair_dim))
    own_branch = branch_pool[0]
    for section_idx in range(section_count):
        branch = spread(own_branch, "slc", owners[section_idx])
        product = jnp.einsum(
            "srab,acb->srcb",
            states.reshape(slice_count, row_total, bond_dim, bond_dim),
            branch.reshape(bond_dim, bond_dim, bond_dim),
            preferred_element_type=jnp.float32,
        )
        table = lax.dynamic_index_in_dim(slice_tensors, tree_order[section_idx], 0, keepdims=False)
        factor = jnp.take(table, slice_assign[:, section_idx], axis=0).astype(jnp.float32)
        states = (product.reshape(slice_count, row_total, pair_dim) * factor[:, None, :]).astype(
            jnp.bfloat16
        )
    inverse = 1.0 / math.sqrt(slice_count * group_count)
    share_rows = row_total // group_count
    partial_amps = jnp.einsum("srw,wo->ro", states, closing, preferred_element_type=jnp.float32)
    totals = lax.psum(partial_amps, "slc")
    summed = lax.dynamic_slice_in_dim(totals, my_index * share_rows, share_rows, 0)
    return summed * inverse


def solution(mesh):
    return jax.shard_map(
        local,
        mesh=mesh,
        in_specs=(
            P("grp"),
            P("grp"),
            P("grp"),
            P(("grp", "slc"), None),
            P("grp", None),
            P(("grp", "slc"), None, None),
            P("grp", None, None),
            P("grp", None),
        ),
        out_specs=P(("grp", "slc"), None),
        check_vma=False,
    )
```

profile of v0, /device:TPU:0, one launch (start us, length us, event | category | flops | bytes accessed | tf_op | source)
XLA Modules:
  0.0 318.7 jit_solution(11319033203107848922)
XLA Ops:
  6.5 1.5 fusion.25
  11.9 2.4 broadcast_select_fusion.6
  14.3 2.1 reshape.99
  16.3 2.9 copy.34
  19.3 2.1 reshape.102
  21.3 2.9 copy.37
  24.2 2.1 reshape.101
  26.3 2.9 copy.36
  29.2 2.1 reshape.100
  31.3 2.9 copy.35
  34.2 1.1 reshape.104
  35.3 2.9 copy.39
  38.2 1.1 reshape.103
  39.4 2.9 copy.38
  42.6 0.7 fusion.24
  55.0 3.2 dynamic-slice_bitcast_fusion.1
  58.2 1.7 gather_fusion.5
  60.2 1.7 gather_fusion.4
  63.1 0.6 gather_fusion.2
  64.8 0.6 gather_fusion.6
  65.7 11.4 %gather_fusion = bf16[512,4096]{1,0:T(8,128)(2,1)} fusion(bf16[512,4096]{1,0:T(8,128)(2,1)} %param.14, s32[1024]{0:T(1024)S(1)} %pad_clamp_fusion.6), kind=kCustom, calls=%fused_computation.6 | custom fusion | bytes 8390656 | tf_op jit(solution)/shard_map/jit(_take)/gather | solution.py:23
  77.1 6.5 %copy.40 = bf16[512,4096]{0,1:T(8,128)(2,1)} copy(bf16[512,4096]{1,0:T(8,128)(2,1)} %gather_fusion) | data formatting | bytes 8388608 | tf_op jit(solution)/shard_map/jit(_take)/gather | solution.py:23
  83.6 2.7 broadcast_select_fusion
  86.3 4.4 %copy.41 = bf16[512,64,64]{0,1,2:T(8,128)(2,1)} copy(bf16[512,64,64]{0,2,1:T(8,128)(2,1)S(1)} %broadcast_select_fusion) | data formatting | bytes 8388608 | tf_op jit(solution)/shard_map/jit(_take)/select_n | solution.py:23
  90.7 94.3 %all-reduce.6.cloned.1.call-done = (bf16[64,64,64]{0,1,2:T(8,128)(2,1)}, bf16[64,64,64]{0,1,2:T(8,128)(2,1)}, bf16[64,64,64]{0,1,2:T(8,128)(2,1)}, bf16[64,64,64...) async-done(((bf16[64,64,64]{0,1,2:T(8,128)(2,1)}, bf16[64,64,64]{0,1,2:T(8,128)(2,1)}, bf16[64,64,64]{0,1,2:T(8,128)(2,1)}, ...) | async-done | bytes 3145744 | tf_op jit(solution)/shard_map/psum | solution.py:10
  185.0 8.7 %fusion.4 = bf16[2,512,64,64]{1,2,0,3:T(8,128)(2,1)} fusion(f32[2,64,64]{1,0,2:T(2,128)S(1)} %copy.43, f32[2,64,64]{1,0,2:T(2,128)S(1)} %copy.42, bf16[512,64,64]{0,1,2:T(8,128)(2,1)} %copy.41, bf16[64,64,64]{0,1,2:T(8,128)(2,1)} %get-tuple-element.12, bf16[64,64,64]{0,1,2:T(8,128)(2,1)} %get-tuple-element.13), kind=kOutput, calls=%fused_computation.16 | convolution fusion | flops 1090519040 | bytes 13697024 | tf_op jit(solution)/shard_map/srab,acb->srcb/dot_general | solution.py:28
  193.7 9.8 %fusion.2 = bf16[2,512,64,64]{1,2,0,3:T(8,128)(2,1)} fusion(f32[2,64,64]{1,0,2:T(2,128)S(1)} %copy.45, bf16[2,512,64,64]{1,2,0,3:T(8,128)(2,1)} %fusion.4, f32[2,64,64]{1,0,2:T(2,128)S(1)} %copy.44, bf16[64,64,64]{0,1,2:T(8,128)(2,1)S(1)} %copy-done.1, bf16[64,64,64]{0,1,2:T(8,128)(2,1)S(1)} %copy-done.2), kind=kOutput, calls=%fused_computation.12 | convolution fusion | flops 1090519040 | bytes 17891328 | tf_op jit(solution)/shard_map/srab,acb->srcb/dot_general | solution.py:28
  203.5 10.4 %convert_reduce_fusion = bf16[512,64,64]{0,1,2:T(8,128)(2,1)} fusion(f32[2,64,64]{1,0,2:T(2,128)S(1)} %copy.47, bf16[2,512,64,64]{1,2,0,3:T(8,128)(2,1)} %fusion.2, f32[2,64,64]{1,0,2:T(2,128)S(1)} %copy.46, bf16[64,64,64]{0,1,2:T(8,128)(2,1)} %get-tuple-element.16, bf16[64,64,64]{0,1,2:T(8,128)(2,1)} %get-tuple-element.17), kind=kOutput, calls=%fused_computation.19 | convolution fusion | flops 1096810496 | bytes 13697024 | tf_op jit(solution)/shard_map/srab,acb->srcb/dot_general | solution.py:28
  213.9 4.5 %copy.48 = bf16[512,64,64]{0,2,1:T(8,128)(2,1)S(1)} copy(bf16[512,64,64]{0,1,2:T(8,128)(2,1)} %convert_reduce_fusion) | data formatting | bytes 8388608 | tf_op jit(solution)/shard_map/srw,wo->ro/reduce_sum | solution.py:41
  218.4 2.0 fusion.26
  220.5 90.1 %all-reduce.4.cloned.1.call-done = f32[512,128]{1,0:T(8,128)} async-done(((f32[512,128]{1,0:T(8,128)}), f32[512,128]{1,0:T(8,128)}) %all-reduce.4.cloned.1.call-update) | async-done | bytes 262160 | tf_op jit(solution)/shard_map/psum | solution.py:42
  310.5 1.3 dynamic-slice_multiply_fusion
  (52 shorter events, 3.5 us)
Async XLA Ops:
  6.5 211.9 %copy-start = (bf16[4096,128]{1,0:T(8,128)(2,1)S(1)}, bf16[4096,128]{1,0:T(8,128)(2,1)}, u32[]{:S(2)}) copy-start(bf16[4096,128]{1,0:T(8,128)(2,1)} %param.17) | copy-start | bytes 3145732
  6.5 178.4 %all-reduce.6.cloned.1.call-start = ((), (), s32[]{:S(2)}) async-start(), calls=%async_computation.1 | async-start | bytes 12582912 | tf_op jit(solution)/shard_map/psum | solution.py:10
  29.2 13.4 %copy-start.4 = (s32[6]{0:T(128)S(1)}, s32[6]{0:T(128)}, u32[]{:S(2)}) copy-start(s32[6]{0:T(128)} %param.11) | copy-start | bytes 76
  29.2 21.6 %copy-start.3 = (s32[2,6]{1,0:T(2,128)S(1)}, s32[2,6]{1,0:T(2,128)}, u32[]{:S(2)}) copy-start(s32[2,6]{1,0:T(2,128)} %param.13) | copy-start | bytes 148
  39.4 26.3 %copy-start.5 = (s32[512]{0:T(512)S(1)}, s32[512]{0:T(512)}, u32[]{:S(2)}) copy-start(s32[512]{0:T(512)} %param.10) | copy-start | bytes 6148
  42.3 268.2 %all-reduce.4.cloned.1.call-start = ((), (), s32[]{:S(2)}) async-start(), calls=%async_computation | async-start | bytes 524288 | tf_op jit(solution)/shard_map/psum | solution.py:42
  185.0 8.7 %copy-start.1 = (bf16[64,64,64]{0,1,2:T(8,128)(2,1)S(1)}, bf16[64,64,64]{0,1,2:T(8,128)(2,1)}, u32[]{:S(2)}) copy-start(bf16[64,64,64]{0,1,2:T(8,128)(2,1)} %get-tuple-element.14) | copy-start | bytes 1572868
  185.0 8.7 %copy-start.2 = (bf16[64,64,64]{0,1,2:T(8,128)(2,1)S(1)}, bf16[64,64,64]{0,1,2:T(8,128)(2,1)}, u32[]{:S(2)}) copy-start(bf16[64,64,64]{0,1,2:T(8,128)(2,1)} %get-tuple-element.15) | copy-start | bytes 1572868
Sparse Core Ops, SparseCore 0:
  42.4 142.4 all-reduce.5
  220.6 89.9 all-reduce.3
where the time goes:
time: 320 us; the launch traced here: 319 us
  waiting for transfers between devices  184 us (58%)
  local copies, waits for them, and re-layouts  67.4 us (21%)
  matrix products  30.9 us (10%)
  between operations  28.8 us (9%)
  other arithmetic  7.02 us (2%)
    psum x1, waiting for transfers between devices, spread(): return lax.psum(block, axis)  94.3 us
    psum x1, waiting for transfers between devices, local(): totals = lax.psum(partial_amps, 'slc')  90.1 us
    dot_general x3, matrix products, local(): jnp.einsum('srab,acb->srcb', states.reshape(slice_count, row_total, bond_...  28.9 us
    reshape x12, local copies, waits for them, and re-layouts, local(): branch.reshape(bond_dim, bond_dim, bond_dim)  28 us
    gather x2, local copies, waits for them, and re-layouts, local(): starts = jnp.take(boundary, bitstrings, axis=0)  17.9 us
  transfers between devices with their start and end apart: 2, of which 2 were waited for; matrix products, arithmetic and copies ran while one was open for 11% of the time, Pallas kernels for 0%

commit v1 on v0

--- a/solution.py
+++ b/solution.py
@@ -3,6 +3,15 @@
 import jax.numpy as jnp
 from jax import lax
 from jax.sharding import PartitionSpec as P
+
+
+def add_in_pairs(array, name):
+    devices = lax.axis_size(name)
+    result, far = (array, 1)
+    while far < devices:
+        result = result + lax.ppermute(result, name, [(i, i ^ far) for i in range(devices)])
+        far = 2 * far
+    return result
 
 
 def spread(block, axis, owner):
@@ -39,7 +48,7 @@
     inverse = 1.0 / math.sqrt(slice_count * group_count)
     share_rows = row_total // group_count
     partial_amps = jnp.einsum("srw,wo->ro", states, closing, preferred_element_type=jnp.float32)
-    totals = lax.psum(partial_amps, "slc")
+    totals = add_in_pairs(partial_amps, "slc")
     summed = lax.dynamic_slice_in_dim(totals, my_index * share_rows, share_rows, 0)
     return summed * inverse
 

time: 320 us -> 259 us (0.81)
  waiting for transfers between devices: 184 us -> 120 us
  starting transfers between devices: 0.22 us -> 5.63 us
    psum x1 -> x0, waiting for transfers between devices: 90.1 us -> none  [local(): totals = lax.psum(partial_amps, 'slc')]
    ppermute x0 -> x4, waiting for transfers between devices: none -> 25.2 us  [add_in_pairs(): lax.ppermute(result, name, [(i, i ^ far) for i in range(devices)])]
    ppermute x0 -> x4, starting transfers between devices: none -> 5.63 us  [add_in_pairs(): lax.ppermute(result, name, [(i, i ^ far) for i in range(devices)])]
  transfers between devices with their start and end apart: 2 -> 5, of which waited for: 2 -> 5; matrix products, arithmetic and copies ran while one was open for 11% -> 14% of each run, Pallas kernels for 0% -> 0%
where the time goes in v1:
time: 259 us; the launch traced here: 258 us
  waiting for transfers between devices  120 us (46%)
  local copies, waits for them, and re-layouts  67.4 us (26%)
  matrix products  30.2 us (12%)
  between operations  28.7 us (11%)
  other arithmetic  6.4 us (2%)
  starting transfers between devices  5.63 us (2%)
    psum x1, waiting for transfers between devices, spread(): return lax.psum(block, axis)  94.4 us
    dot_general x3, matrix products, local(): jnp.einsum('srab,acb->srcb', states.reshape(slice_count, row_total, bond_...  28.9 us
    reshape x12, local copies, waits for them, and re-layouts, local(): branch.reshape(bond_dim, bond_dim, bond_dim)  28 us
    ppermute x4, waiting for transfers between devices, add_in_pairs(): lax.ppermute(result, name, [(i, i ^ far) for i in range(devices)])  25.2 us
    gather x2, local copies, waits for them, and re-layouts, local(): starts = jnp.take(boundary, bitstrings, axis=0)  17.9 us
    gather x6, local copies, waits for them, and re-layouts, local(): jnp.take(table, slice_assign[:, section_idx], axis=0).astype(jnp.float32)  5.73 us
    ppermute x4, starting transfers between devices, add_in_pairs(): lax.ppermute(result, name, [(i, i ^ far) for i in range(devices)])  5.63 us
  transfers between devices with their start and end apart: 5, of which 5 were waited for; matrix products, arithmetic and copies ran while one was open for 14% of the time, Pallas kernels for 0%

profile of v1, /device:TPU:0, one launch (start us, length us, event | category | flops | bytes accessed | tf_op | source)
XLA Modules:
  0.0 257.9 jit_solution(15394394379374392885)
XLA Ops:
  6.5 1.6 fusion.26
  11.9 2.4 broadcast_select_fusion.6
  14.3 2.1 reshape.99
  16.3 2.9 %copy.34 = bf16[64,64,64]{0,1,2:T(8,128)(2,1)} copy(bf16[64,64,64]{2,1,0:T(8,128)(2,1)S(1)} %reshape.99) | data formatting | bytes 1048576 | tf_op jit(solution)/shard_map/reshape | solution.py:40
  19.2 2.1 reshape.102
  21.3 2.9 %copy.37 = bf16[64,64,64]{0,1,2:T(8,128)(2,1)} copy(bf16[64,64,64]{2,1,0:T(8,128)(2,1)S(1)} %reshape.102) | data formatting | bytes 1048576 | tf_op jit(solution)/shard_map/reshape | solution.py:40
  24.2 2.1 reshape.101
  26.3 2.9 %copy.36 = bf16[64,64,64]{0,1,2:T(8,128)(2,1)} copy(bf16[64,64,64]{2,1,0:T(8,128)(2,1)S(1)} %reshape.101) | data formatting | bytes 1048576 | tf_op jit(solution)/shard_map/reshape | solution.py:40
  29.2 2.1 reshape.100
  31.3 2.9 %copy.35 = bf16[64,64,64]{0,1,2:T(8,128)(2,1)} copy(bf16[64,64,64]{2,1,0:T(8,128)(2,1)S(1)} %reshape.100) | data formatting | bytes 1048576 | tf_op jit(solution)/shard_map/reshape | solution.py:40
  35.3 2.9 %copy.39 = bf16[64,64,64]{0,1,2:T(8,128)(2,1)} copy(bf16[64,64,64]{2,1,0:T(8,128)(2,1)S(1)} %reshape.104) | data formatting | bytes 1048576 | tf_op jit(solution)/shard_map/reshape | solution.py:40
  39.4 2.9 %copy.38 = bf16[64,64,64]{0,1,2:T(8,128)(2,1)} copy(bf16[64,64,64]{2,1,0:T(8,128)(2,1)S(1)} %reshape.103) | data formatting | bytes 1048576 | tf_op jit(solution)/shard_map/reshape | solution.py:40
  54.8 3.1 %dynamic-slice_bitcast_fusion.1 = (bf16[64,4096]{1,0:T(8,128)(2,1)}, bf16[64,4096]{1,0:T(8,128)(2,1)}, bf16[64,4096]{1,0:T(8,128)(2,1)S(1)}, bf16[64,4096]{1,0:T...) fusion(bf16[6,64,4096]{2,1,0:T(8,128)(2,1)} %param.16, s32[]{:T(128)S(6)} %select_n.122, ...), kind=kLoop, calls=%fused_computation.29 | loop fusion | bytes 6291480 | tf_op jit(solution)/shard_map/jit(dynamic_index_in_dim)/squeeze | solution.py:43
  57.9 1.7 gather_fusion.5
  59.9 1.7 gather_fusion.4
  65.4 11.4 %gather_fusion = bf16[512,4096]{1,0:T(8,128)(2,1)} fusion(bf16[512,4096]{1,0:T(8,128)(2,1)} %param.14, s32[1024]{0:T(1024)S(1)} %pad_clamp_fusion.6), kind=kCustom, calls=%fused_computation.6 | custom fusion | bytes 8390656 | tf_op jit(solution)/shard_map/jit(_take)/gather | solution.py:32
  76.8 6.6 %copy.40 = bf16[512,4096]{0,1:T(8,128)(2,1)} copy(bf16[512,4096]{1,0:T(8,128)(2,1)} %gather_fusion) | data formatting | bytes 8388608 | tf_op jit(solution)/shard_map/jit(_take)/gather | solution.py:32
  83.3 2.7 %broadcast_select_fusion = bf16[512,64,64]{0,2,1:T(8,128)(2,1)S(1)} fusion(bf16[512,64,64]{0,2,1:T(8,128)(2,1)} %bitcast.97, pred[512]{0:T(512)(128)(4,1)S(1)} %compare_and_fusion.6), kind=kLoop, calls=%fused_computation.21 | loop fusion | flops 2097152 | bytes 8389120 | tf_op jit(solution)/shard_map/jit(_take)/select_n | solution.py:32
  86.0 4.4 %copy.41 = bf16[512,64,64]{0,1,2:T(8,128)(2,1)} copy(bf16[512,64,64]{0,2,1:T(8,128)(2,1)S(1)} %broadcast_select_fusion) | data formatting | bytes 8388608 | tf_op jit(solution)/shard_map/jit(_take)/select_n | solution.py:32
  90.4 94.4 %all-reduce.3.cloned.1.call-done = (bf16[64,64,64]{0,1,2:T(8,128)(2,1)}, bf16[64,64,64]{0,1,2:T(8,128)(2,1)}, bf16[64,64,64]{0,1,2:T(8,128)(2,1)}, bf16[64,64,64...) async-done(((bf16[64,64,64]{0,1,2:T(8,128)(2,1)}, bf16[64,64,64]{0,1,2:T(8,128)(2,1)}, bf16[64,64,64]{0,1,2:T(8,128)(2,1)}, ...) | async-done | bytes 3145744 | tf_op jit(solution)/shard_map/psum | solution.py:19
  184.8 8.7 %fusion.4 = bf16[2,512,64,64]{1,2,0,3:T(8,128)(2,1)} fusion(f32[2,64,64]{1,0,2:T(2,128)S(1)} %copy.43, f32[2,64,64]{1,0,2:T(2,128)S(1)} %copy.42, bf16[512,64,64]{0,1,2:T(8,128)(2,1)} %copy.41, bf16[64,64,64]{0,1,2:T(8,128)(2,1)} %get-tuple-element.12, bf16[64,64,64]{0,1,2:T(8,128)(2,1)} %get-tuple-element.13), kind=kOutput, calls=%fused_computation.16 | convolution fusion | flops 1090519040 | bytes 13697024 | tf_op jit(solution)/shard_map/srab,acb->srcb/dot_general | solution.py:37
  193.5 10.0 %fusion.2 = bf16[2,512,64,64]{1,2,0,3:T(8,128)(2,1)} fusion(f32[2,64,64]{1,0,2:T(2,128)S(1)} %copy.45, bf16[2,512,64,64]{1,2,0,3:T(8,128)(2,1)} %fusion.4, f32[2,64,64]{1,0,2:T(2,128)S(1)} %copy.44, bf16[64,64,64]{0,1,2:T(8,128)(2,1)S(1)} %copy-done.1, bf16[64,64,64]{0,1,2:T(8,128)(2,1)S(1)} %copy-done.2), kind=kOutput, calls=%fused_computation.12 | convolution fusion | flops 1090519040 | bytes 17891328 | tf_op jit(solution)/shard_map/srab,acb->srcb/dot_general | solution.py:37
  203.5 10.2 %convert_reduce_fusion = bf16[512,64,64]{0,1,2:T(8,128)(2,1)} fusion(f32[2,64,64]{1,0,2:T(2,128)S(1)} %copy.47, bf16[2,512,64,64]{1,2,0,3:T(8,128)(2,1)} %fusion.2, f32[2,64,64]{1,0,2:T(2,128)S(1)} %copy.46, bf16[64,64,64]{0,1,2:T(8,128)(2,1)} %get-tuple-element.16, bf16[64,64,64]{0,1,2:T(8,128)(2,1)} %get-tuple-element.17), kind=kOutput, calls=%fused_computation.19 | convolution fusion | flops 1096810496 | bytes 13697024 | tf_op jit(solution)/shard_map/srab,acb->srcb/dot_general | solution.py:37
  213.7 4.5 %copy.48 = bf16[512,64,64]{0,2,1:T(8,128)(2,1)S(1)} copy(bf16[512,64,64]{0,1,2:T(8,128)(2,1)} %convert_reduce_fusion) | data formatting | bytes 8388608 | tf_op jit(solution)/shard_map/srw,wo->ro/reduce_sum | solution.py:50
  218.3 1.3 fusion.27
  219.6 1.5 collective-permute-done
  221.2 1.5 collective-permute-start.1
  222.7 6.9 %collective-permute-done.1 = f32[512,128]{1,0:T(8,128)S(1)} collective-permute-done((f32[512,128]{1,0:T(8,128)S(1)}, f32[512,128]{1,0:T(8,128)S(1)}, u32[]{:S(2)}, u32[]{:S(2)}) %collective-permute-start.1) | collective-permute-done | bytes 262176 | tf_op jit(solution)/shard_map/ppermute | solution.py:12
  229.6 1.6 collective-permute-start.2
  231.2 6.0 %collective-permute-done.2 = f32[512,128]{1,0:T(8,128)S(1)} collective-permute-done((f32[512,128]{1,0:T(8,128)S(1)}, f32[512,128]{1,0:T(8,128)S(1)}, u32[]{:S(2)}, u32[]{:S(2)}) %collective-permute-start.2) | collective-permute-done | bytes 262176 | tf_op jit(solution)/shard_map/ppermute | solution.py:12
  237.2 2.5 collective-permute-start.3
  239.7 10.8 %collective-permute-done.3 = f32[512,128]{1,0:T(8,128)S(1)} collective-permute-done((f32[512,128]{1,0:T(8,128)S(1)}, f32[512,128]{1,0:T(8,128)S(1)}, u32[]{:S(2)}, u32[]{:S(2)}) %collective-permute-start.3) | collective-permute-done | bytes 262176 | tf_op jit(solution)/shard_map/ppermute | solution.py:12
  (60 shorter events, 8.1 us)
Async XLA Ops:
  6.5 211.7 %copy-start = (bf16[4096,128]{1,0:T(8,128)(2,1)S(1)}, bf16[4096,128]{1,0:T(8,128)(2,1)}, u32[]{:S(2)}) copy-start(bf16[4096,128]{1,0:T(8,128)(2,1)} %param.17) | copy-start | bytes 3145732
  6.5 178.3 %all-reduce.3.cloned.1.call-start = ((), (), s32[]{:S(2)}) async-start(), calls=%async_computation | async-start | bytes 12582912 | tf_op jit(solution)/shard_map/psum | solution.py:19
  29.2 13.2 %copy-start.4 = (s32[6]{0:T(128)S(1)}, s32[6]{0:T(128)}, u32[]{:S(2)}) copy-start(s32[6]{0:T(128)} %param.11) | copy-start | bytes 76
  29.2 21.4 %copy-start.3 = (s32[2,6]{1,0:T(2,128)S(1)}, s32[2,6]{1,0:T(2,128)}, u32[]{:S(2)}) copy-start(s32[2,6]{1,0:T(2,128)} %param.13) | copy-start | bytes 148
  39.4 26.0 %copy-start.5 = (s32[512]{0:T(512)S(1)}, s32[512]{0:T(512)}, u32[]{:S(2)}) copy-start(s32[512]{0:T(512)} %param.10) | copy-start | bytes 6148
  184.8 8.7 %copy-start.1 = (bf16[64,64,64]{0,1,2:T(8,128)(2,1)S(1)}, bf16[64,64,64]{0,1,2:T(8,128)(2,1)}, u32[]{:S(2)}) copy-start(bf16[64,64,64]{0,1,2:T(8,128)(2,1)} %get-tuple-element.14) | copy-start | bytes 1572868
  184.8 8.7 %copy-start.2 = (bf16[64,64,64]{0,1,2:T(8,128)(2,1)S(1)}, bf16[64,64,64]{0,1,2:T(8,128)(2,1)}, u32[]{:S(2)}) copy-start(bf16[64,64,64]{0,1,2:T(8,128)(2,1)} %get-tuple-element.15) | copy-start | bytes 1572868
  219.6 1.6 collective-permute-start
  221.2 8.4 %collective-permute-start.1 = (f32[512,128]{1,0:T(8,128)S(1)}, f32[512,128]{1,0:T(8,128)S(1)}, u32[]{:S(2)}, u32[]{:S(2)}) collective-permute-start(f32[512,128]{1,0:T(8,128)S(1)} %add.65), channel_id=1, source_target_pairs={{0,2},{1,3},{2,0},{3,1},{4,6},{5,7},{6,4},{7,5},{8,10},{9,11},{10,... | collective-permute-start | bytes 786440 | tf_op jit(solution)/shard_map/ppermute | solution.py:12
  229.6 7.6 %collective-permute-start.2 = (f32[512,128]{1,0:T(8,128)S(1)}, f32[512,128]{1,0:T(8,128)S(1)}, u32[]{:S(2)}, u32[]{:S(2)}) collective-permute-start(f32[512,128]{1,0:T(8,128)S(1)} %add.66), channel_id=1, source_target_pairs={{0,4},{1,5},{2,6},{3,7},{4,0},{5,1},{6,2},{7,3},{8,12},{9,13},{10,... | collective-permute-start | bytes 786440 | tf_op jit(solution)/shard_map/ppermute | solution.py:12
  237.2 13.2 %collective-permute-start.3 = (f32[512,128]{1,0:T(8,128)S(1)}, f32[512,128]{1,0:T(8,128)S(1)}, u32[]{:S(2)}, u32[]{:S(2)}) collective-permute-start(f32[512,128]{1,0:T(8,128)S(1)} %add.67), channel_id=1, source_target_pairs={{0,8},{1,9},{2,10},{3,11},{4,12},{5,13},{6,14},{7,15},{8,0},{9,1},... | collective-permute-start | bytes 786440 | tf_op jit(solution)/shard_map/ppermute | solution.py:12
Sparse Core Ops, SparseCore 0:
  42.5 142.2 all-reduce.2
